TPU v7x, 256 devices: a whole 4x4x8 slice. The times are simulated.
256 devices in a mesh: ctx: 32 (over y, z), head: 8 (over x, core).
Axes of the slice: x: 4, y: 4, z: 8, core: 2. Of those that a mesh axis runs over, the one named last changes fastest.
Arguments:
- queries: bfloat16 [16384, 2048], P('ctx', 'head'), may hold values from -4.5 to 4.5
- keys: bfloat16 [16384, 1024], P('ctx', 'head'), may hold values from -4.5 to 4.5
- values: bfloat16 [16384, 1024], P('ctx', 'head'), may hold values from -4.5 to 4.5
- offsets: int32 [32], P('ctx'), may hold values from 0 to 512, as said below
- gate_logits: float32 [16], P('head'), may hold values from -2 to 2
- out_weight: bfloat16 [2048, 2048], P('head'), may hold values from -0.125 to 0.125
- grad_mixed: bfloat16 [16384, 2048], P('ctx', 'head'), may hold values from -6 to 6
Outputs:
- mixed: bfloat16 [16384, 2048], P('ctx', 'head')
- grad_queries: float32 [16384, 2048], P('ctx', 'head')
- grad_keys: float32 [16384, 1024], P('ctx', 'head')
- grad_values: float32 [16384, 1024], P('ctx', 'head')
- grad_weight: float32 [2048, 2048], P('head', 'ctx')
- grad_gates: float32 [16], P('head')
Inputs may be any that keep to these rules, and one draw needn't show every extreme that they name: `offsets`: entry s is 512 where segment s continues the document of the segment before it, else the position within segment s at which a new document begins.
All inputs are finite; a program needn't handle non-finite values.
Results may differ from a plain program's by a relative error of at most 0.0064.
Values may be sent and summed in bfloat16 or wider, within the bound.
No kernel may reach another device: no remote copies, remote signals or barrier semaphores. Data moves between devices by JAX's collectives and lax.ppermute only.
A program may use at most 64 MiB of HBM per device.

v0:
```python
import jax
import jax.numpy as jnp
from jax import lax
from jax.sharding import Mesh
from jax.sharding import PartitionSpec as P

HEAD_DIM = 128
SEG = 512
CTX = ("ctx_0", "ctx_1")
HEAD = ("head_0", "head_1")
highest = lax.Precision.HIGHEST


def neutral_like(value, identity):
    return jax.tree.map(
        lambda a, e: jnp.broadcast_to(jnp.asarray(e, a.dtype), a.shape), value, identity
    )


def collected_together(value, axis):
    leaves = jax.tree.leaves(value)
    order = sorted(range(len(leaves)), key=lambda k: -leaves[k].size)
    width = (1, *leaves[order[0]].shape)[-1]
    lines = [
        jnp.pad(leaves[k].reshape(-1), (0, -leaves[k].size % width)).reshape(-1, width)
        for k in order
    ]
    both, at, found = (lax.all_gather(jnp.concatenate(lines), axis), 0, {})
    for k, line in zip(order, lines):
        slab = both[:, at : at + len(line)].reshape(len(both), -1)
        found[k] = slab[:, : leaves[k].size].reshape(-1, *leaves[k].shape)
        at += len(line)
    numbers = iter(range(len(leaves)))
    return jax.tree.map(lambda _: found[next(numbers)], value)


def entering(value, axes, combine, identity):
    before = start = neutral_like(value, identity)
    running = value
    for axis in reversed(axes):
        size, index = (lax.axis_size(axis), lax.axis_index(axis))
        pieces = collected_together(running, axis)
        inside, running = (start, start)
        for k in range(size):
            passed = k < index
            running = combine(running, jax.tree.map(lambda part: part[k], pieces))
            inside = jax.tree.map(lambda new, old: jnp.where(passed, new, old), running, inside)
        before = combine(inside, before)
    return before


def piece_ends(length, count):
    unit = 8 if length >= 8 * count else 1
    return [length // unit * k // count * unit for k in range(1, count)]


def gather_in_order(value, axes, order):
    parts = value[None]
    for k in order:
        parts = lax.all_gather(parts, axes[k], axis=0, tiled=True)
    current = [lax.axis_size(axes[k]) for k in reversed(order)]
    parts = parts.reshape(*current, *value.shape)
    turned = sorted(range(len(order)), key=lambda place: order[len(order) - 1 - place])
    return parts.transpose(*turned, *range(len(order), parts.ndim)).reshape(-1, *value.shape)


def laid_out(parts, dim):
    dims = list(parts.shape[1:])
    dims[dim] *= parts.shape[0]
    return jnp.moveaxis(parts, 0, dim).reshape(dims)


def spread_gather(value, axes, dim):
    numbers = list(range(len(axes)))[::-1]
    cut = value.shape.index(max(value.shape[:-1] or value.shape))
    edges = [0, *piece_ends(value.shape[cut], len(axes)), value.shape[cut]]
    outs = []
    for k, (start, end) in enumerate(zip(edges, edges[1:])):
        if end > start:
            slab = lax.slice_in_dim(value, start, end, axis=cut)
            outs.append(gather_in_order(slab, axes, numbers[k:] + numbers[:k]))
    return laid_out(jnp.concatenate(outs, axis=cut + 1), dim)


def copy_for_each(value, axis):
    copies = jnp.broadcast_to(value, (lax.axis_size(axis), *value.shape))
    return lax.all_to_all(copies, axis, split_axis=0, concat_axis=0, tiled=True)


def collect(value, axis, dim):
    return laid_out(copy_for_each(value, axis), dim)


def cut_along(value, dim, size):
    before, after = (value.shape[:dim], value.shape[dim + 1 :])
    return jnp.moveaxis(value.reshape(*before, size, -1, *after), dim, 0)


def sent_and_summed(value, axis, dim):
    parts = cut_along(value, dim, lax.axis_size(axis))
    arrived = lax.all_to_all(parts, axis, split_axis=0, concat_axis=0, tiled=True)
    return arrived.sum(axis=0)


def gathered_by_type(value, axis):
    leaves, found = (jax.tree.leaves(value), {})
    for leading, a in enumerate(leaves):
        if leading not in found:
            alike = [k for k, b in enumerate(leaves) if b.dtype == a.dtype]
            got = (
                collected_together([leaves[k] for k in alike], axis)
                if len(alike) > 1
                else [lax.all_gather(a, axis)]
            )
            for k, b in zip(alike, got):
                found[k] = b
    numbers = iter(range(len(leaves)))
    return jax.tree.map(lambda _: found[next(numbers)], value)


def entering_2(value, axes, combine, identity):
    before = start = neutral_like(value, identity)
    running = value
    for axis in reversed(axes):
        size, index = (lax.axis_size(axis), lax.axis_index(axis))
        pieces = gathered_by_type(running, axis)
        inside, running = (start, start)
        for k in reversed(range(size)):
            passed = k > index
            running = combine(running, jax.tree.map(lambda part: part[k], pieces))
            inside = jax.tree.map(lambda new, old: jnp.where(passed, new, old), running, inside)
        before = combine(inside, before)
    return before


def of_everyone(value, axis):
    return copy_for_each(value, axis).sum(axis=0)


def feature(inputs):
    return jnp.where(inputs > 0, inputs + 1.0, jnp.exp(jnp.minimum(inputs, 0.0)))


def feature_slope(inputs):
    return jnp.where(inputs > 0, 1.0, jnp.exp(jnp.minimum(inputs, 0.0)))


def compose(earlier, later):
    return (
        later[2][:, None, None] * earlier[0] + later[0],
        later[2][:, None] * earlier[1] + later[1],
        earlier[2] * later[2],
    )


def segment_element(memory, totals, factor, segment):
    return (memory[segment], totals[segment], factor)


def body(queries, keys, values, offsets, gate_logits, out_weight, grad_mixed):
    tokens = queries.shape[0]
    head_count = queries.shape[1] // HEAD_DIM
    groups = keys.shape[1] // HEAD_DIM
    repeat = head_count // groups
    segments = tokens // SEG
    score_scale = HEAD_DIM ** (-0.5)
    query_blocks = queries.reshape(segments, SEG, groups, repeat, HEAD_DIM)
    key_blocks = keys.reshape(segments, SEG, groups, HEAD_DIM)
    value_blocks = values.reshape(segments, SEG, groups, HEAD_DIM)
    query_float = query_blocks.astype(jnp.float32)
    key_float = key_blocks.astype(jnp.float32)
    value_float = value_blocks.astype(jnp.float32)
    query_feat = feature(query_float)
    key_feat = feature(key_float)
    position = jnp.arange(SEG)
    retain = (position[None, :] < offsets[:, None]).astype(jnp.float32)
    start_cut = jnp.where(offsets == SEG, 0, offsets)
    counted = (position[None, :] >= start_cut[:, None]).astype(jnp.float32)
    carry_factor = (offsets == SEG).astype(jnp.float32)
    counted_feat = key_feat * counted[:, :, None, None]
    delta_memory = jnp.einsum("sjgd,sjge->sgde", counted_feat, value_float, precision=highest)
    delta_totals = jnp.sum(counted_feat, axis=1)
    identity = (
        jnp.zeros((groups, HEAD_DIM, HEAD_DIM), jnp.float32),
        jnp.zeros((groups, HEAD_DIM), jnp.float32),
        jnp.ones((1,), jnp.float32),
    )
    device_element = identity
    segment = 0
    device_element = compose(
        device_element, segment_element(delta_memory, delta_totals, carry_factor, segment)
    )
    incoming = entering(device_element, CTX, compose, identity)
    running = incoming
    segment = 0
    memory_list = [running[0]]
    totals_list = [running[1]]
    memory_in = jnp.stack(memory_list)
    totals_in = jnp.stack(totals_list)
    retained_feat = query_feat * retain[:, :, None, None, None]
    numerator = jnp.einsum("sigrd,sgde->sigre", retained_feat, memory_in, precision=highest)
    denominator = 1.0 + jnp.einsum("sigrd,sgd->sigr", retained_feat, totals_in, precision=highest)
    recall = numerator / denominator[..., None]
    scores = (
        jnp.einsum(
            "sigrd,sjgd->sgrij", query_blocks, key_blocks, preferred_element_type=jnp.float32
        )
        * score_scale
    )
    later_doc = position[None, :] >= offsets[:, None]
    allowed = (position[None, None, :] <= position[None, :, None]) & (
        later_doc[:, :, None] == later_doc[:, None, :]
    )
    scores = jnp.where(allowed[:, None, None], scores, -1e30)
    scaled_exp = jnp.exp(scores - jnp.max(scores, axis=-1, keepdims=True))
    weights = scaled_exp / jnp.sum(scaled_exp, axis=-1, keepdims=True)
    weights_low = weights.astype(jnp.bfloat16)
    attend = jnp.einsum(
        "sgrij,sjgd->sigrd", weights_low, value_blocks, preferred_element_type=jnp.float32
    )
    sigmoid_gate = jax.nn.sigmoid(gate_logits).reshape(groups, repeat)
    mixing = sigmoid_gate[None, None, :, :, None]
    output = (mixing * recall + (1.0 - mixing) * attend).astype(jnp.bfloat16)
    out_flat = output.reshape(tokens, head_count * HEAD_DIM)
    gathered = spread_gather(out_flat, HEAD, 1)
    weight_cols = lax.all_to_all(out_weight, HEAD, split_axis=1, concat_axis=0, tiled=True)
    mixed = jnp.dot(gathered, weight_cols, preferred_element_type=jnp.float32).astype(jnp.bfloat16)
    cotangent = collect(grad_mixed, HEAD, 1)
    grad_output = lax.dot_general(
        cotangent, out_weight, (((1,), (1,)), ((), ())), preferred_element_type=jnp.float32
    ).astype(jnp.bfloat16)
    weight_terms = lax.dot_general(
        out_flat, cotangent, (((0,), (0,)), ((), ())), preferred_element_type=jnp.float32
    )
    grad_weight = sent_and_summed(weight_terms, CTX, 1)
    grad_blocks = grad_output.reshape(segments, SEG, groups, repeat, HEAD_DIM)
    grad_float = grad_blocks.astype(jnp.float32)
    gate_slope = sigmoid_gate * (1.0 - sigmoid_gate)
    gate_terms = (jnp.sum(grad_float * (recall - attend), axis=(0, 1, 4)) * gate_slope).reshape(
        head_count
    )
    grad_recall = mixing * grad_float
    complement = (1.0 - sigmoid_gate)[None, :, :, None, None]
    grad_probs = complement * jnp.einsum(
        "sigrd,sjgd->sgrij", grad_blocks, value_blocks, preferred_element_type=jnp.float32
    )
    grad_scores = (
        weights * (grad_probs - jnp.sum(grad_probs * weights, axis=-1, keepdims=True)) * score_scale
    )
    grad_low = grad_scores.astype(jnp.bfloat16)
    grad_query = jnp.einsum(
        "sgrij,sjgd->sigrd", grad_low, key_blocks, preferred_element_type=jnp.float32
    )
    grad_key = jnp.einsum(
        "sgrij,sigrd->sjgd", grad_low, query_blocks, preferred_element_type=jnp.float32
    )
    value_terms = jnp.einsum(
        "sgrij,sigrd->sjgrd", weights_low, grad_blocks, preferred_element_type=jnp.float32
    )
    grad_value = jnp.sum(value_terms * (1.0 - sigmoid_gate)[None, None, :, :, None], axis=3)
    grad_numer = grad_recall / denominator[..., None]
    grad_denom = -jnp.sum(grad_recall * numerator, axis=-1) / (denominator * denominator)
    grad_feat = retain[:, :, None, None, None] * (
        jnp.einsum("sigre,sgde->sigrd", grad_numer, memory_in, precision=highest)
        + grad_denom[..., None] * totals_in[:, None, :, None, :]
    )
    grad_memory = jnp.einsum("sigrd,sigre->sgde", retained_feat, grad_numer, precision=highest)
    grad_totals = jnp.einsum("sigr,sigrd->sgd", grad_denom, retained_feat, precision=highest)
    grad_queries = (grad_query + grad_feat * feature_slope(query_float)).reshape(
        tokens, head_count * HEAD_DIM
    )
    device_grad = identity
    for segment in reversed(range(segments)):
        device_grad = compose(
            device_grad, segment_element(grad_memory, grad_totals, carry_factor, segment)
        )
    flowing = entering_2(device_grad, CTX, compose, identity)
    running = flowing
    flow_list = []
    flow_totals_list = []
    for segment in reversed(range(segments)):
        flow_list.append(running[0])
        flow_totals_list.append(running[1])
        running = compose(running, segment_element(grad_memory, grad_totals, carry_factor, segment))
    flow_memory = jnp.stack(flow_list[::-1])
    flow_totals = jnp.stack(flow_totals_list[::-1])
    counted_wide = counted[:, :, None, None]
    grad_key_feat = counted_wide * (
        jnp.einsum("sjge,sgde->sjgd", value_float, flow_memory, precision=highest)
        + flow_totals[:, None, :, :]
    )
    grad_keys = (grad_key + grad_key_feat * feature_slope(key_float)).reshape(
        tokens, groups * HEAD_DIM
    )
    grad_value_mem = counted_wide * jnp.einsum(
        "sjgd,sgde->sjge", key_feat, flow_memory, precision=highest
    )
    grad_values = (grad_value + grad_value_mem).reshape(tokens, groups * HEAD_DIM)
    grad_gates = of_everyone(gate_terms, CTX)
    return (mixed, grad_queries, grad_keys, grad_values, grad_weight, grad_gates)


def solution(mesh):
    torus = Mesh(mesh.devices.reshape(4, 8, 4, 2), ("ctx_0", "ctx_1", "head_0", "head_1"))
    in_specs = (
        P(CTX, HEAD),
        P(CTX, HEAD),
        P(CTX, HEAD),
        P(CTX),
        P(HEAD),
        P(HEAD, None),
        P(CTX, HEAD),
    )
    out_specs = (P(CTX, HEAD), P(CTX, HEAD), P(CTX, HEAD), P(CTX, HEAD), P(HEAD, CTX), P(HEAD))
    return jax.shard_map(body, mesh=torus, in_specs=in_specs, out_specs=out_specs, check_vma=False)
```

profile of v0, /device:TPU:8, one launch (start us, length us, event | category | flops | bytes accessed | tf_op | source)
XLA Modules:
  0.0 258.9 jit_solution(9639778417188686132)
XLA Ops:
  9.8 4.4 %all-to-all-start.1 = ((bf16[8,512,256]{1,2,0:T(8,128)(2,1)}), bf16[8,512,256]{1,2,0:T(8,128)(2,1)S(1)}, u32[]{:S(2)}, u32[]{:S(2)}) async-start(bf16[8,512,256]{1,2,0:T(8,128)(2,1)} %broadcast_in_dim.34), calls=%async_computation.1 | async-start | bytes 4194304 | tf_op jit(solution)/shard_map/all_to_all | solution.py:87
  15.7 29.1 %all-gather.4 = f32[8,130,128]{2,1,0:T(8,128)S(1)} all-gather(f32[1,130,128]{2,1,0:T(8,128)S(1)} %fusion.61), channel_id=2, replica_groups=mesh['ctx_0'=4,'ctx_1'=8,'head_0'=4,'head_1'=2] {'ctx_1'}, dimensions={0}, use_global_device_ids=true | all-gather | bytes 599040 | tf_op jit(solution)/shard_map/all_gather | solution.py:28
  46.1 4.9 %slice_add_fusion.16 = (f32[1,128,128]{2,1,0:T(8,128)S(1)}, f32[1,128,128]{2,1,0:T(8,128)}) fusion(f32[8,130,128]{2,1,0:T(8,128)S(1)} %all-gather.4, f32[]{:T(128)} %bitcast.23, f32[]{:T(128)} %bitcast.22, f32[]{:T(128)} %bitcast.25, f32[]{:T(128)} %bitcast.24, f32[]{:T(128)} %bitcast.29, f32[]{:T(128)} %bitcast.28, f32[]{:T(128)} %bitcast.27, f32[]{:T(128)} %bitcast.26), kind=kLoop, calls=%fused_computation.120 | loop fusion | flops 245760 | bytes 655392 | tf_op jit(solution)/shard_map/add | solution.py:150
  51.0 4.3 %slice_add_fusion.40 = (f32[1,1,128]{2,1,0:T(1,128)S(1)}, f32[1,1,128]{2,1,0:T(1,128)S(1)}, f32[1,1,128]{2,1,0:T(1,128)S(1)}) fusion(f32[8,130,128]{2,1,0:T(8,128)S(1)} %all-gather.4, f32[]{:T(128)} %bitcast.22, f32[]{:T(128)} %bitcast.23, f32[]{:T(128)} %bitcast.25, f32[]{:T(128)} %bitcast.24, f32[]{:T(128)} %bitcast.29, f32[]{:T(128)} %bitcast.28, ...), kind=kLoop, calls=%fused_computation.179 | loop fusion | flops 1920 | bytes 5664 | tf_op jit(solution)/shard_map/add | solution.py:151
  60.3 12.8 %all-gather.5 = f32[4,130,128]{2,1,0:T(8,128)S(1)} all-gather(f32[1,130,128]{2,1,0:T(8,128)S(1)} %maximum_bitcast_fusion.6), channel_id=3, replica_groups=mesh['ctx_0'=4,'ctx_1'=8,'head_0'=4,'head_1'=2] {'ctx_0'}, dimensions={0}, use_global_device_ids=true | all-gather | bytes 332800 | tf_op jit(solution)/shard_map/all_gather | solution.py:28
  77.7 5.7 %bitcast_add_fusion.2 = (f32[128]{0:T(128)}, f32[1,1,128]{2,1,0:T(1,128)S(1)}, f32[1,1,128]{2,1,0:T(1,128)S(1)}) fusion(f32[1,1,128]{2,1,0:T(1,128)S(1)} %get-tuple-element.48, f32[1,1,128]{2,1,0:T(1,128)S(1)} %get-tuple-element.49, f32[1,1,128]{2,1,0:T(1,128)S(1)} %get-tuple-element.50, pred[]{:T(512)} %gt.71, pred[]{:T(512)} %gt.70, ...), kind=kLoop, calls=%fused_computation.190 | loop fusion | flops 3840 | bytes 7732 | tf_op jit(solution)/shard_map/add | solution.py:151
  83.3 1.8 fusion.76
  86.4 2.1 copy.134
  88.4 2.3 copy.127
  90.7 2.3 copy.128
  92.9 6.2 %fusion.70 = f32[128,128,1]{1,0,2:T(8,128)S(1)} fusion(f32[4,130,128]{2,1,0:T(8,128)} %copy-done.11, f32[1,128,128]{2,1,0:T(8,128)} %copy-done.15, f32[1,128,128]{2,1,0:T(8,128)} %get-tuple-element.47, f32[8,130,128]{2,1,0:T(8,128)} %copy-done.7, f32[]{:T(128)} %bitcast.38, f32[]{:T(128)} %bitcast.37, f32[]{:T(128)} %bitcast.36, f32[]{:T(128)} %bitcast.35, ...), kind=kLoop, calls=%fused_computation.116 | loop fusion | flops 524288 | bytes 852024 | tf_op jit(solution)/shard_map/reshape.106
  102.7 4.4 %all-to-all-start = ((bf16[256,8,256]{2,0,1:T(8,128)(2,1)}), bf16[256,8,256]{2,0,1:T(8,128)(2,1)}, u32[]{:S(2)}, u32[]{:S(2)}) async-start(bf16[256,8,256]{2,0,1:T(8,128)(2,1)} %copy.128), calls=%async_computation | async-start | bytes 2097152 | tf_op jit(solution)/shard_map/all_to_all | solution.py:226
  107.1 2.1 bitcast_divide_fusion
  112.4 2.1 convolution_bitcast_fusion
  114.4 8.7 %all-to-all-done = bf16[256,8,256]{2,0,1:T(8,128)(2,1)} async-done(((bf16[256,8,256]{2,0,1:T(8,128)(2,1)}), bf16[256,8,256]{2,0,1:T(8,128)(2,1)}, u32[]{:S(2)}, u32[]{:S(2)}) %all-to-all-start) | async-done | bytes 1048608 | tf_op jit(solution)/shard_map/all_to_all | solution.py:226
  123.8 7.8 %all-to-all-start.3 = ((f32[32,1,2]{2,1,0:T(1,128)}), f32[32,1,2]{2,1,0:T(1,128)S(1)}, u32[]{:S(2)}, u32[]{:S(2)}) async-start(f32[32,1,2]{2,1,0:T(1,128)} %broadcast_in_dim.35), calls=%async_computation.3 | async-start | bytes 32768 | tf_op jit(solution)/shard_map/all_to_all | solution.py:87
  131.6 26.8 %all-gather.6 = f32[8,130,128]{2,1,0:T(8,128)S(1)} all-gather(f32[1,130,128]{2,1,0:T(8,128)} %fusion.62), channel_id=4, replica_groups=mesh['ctx_0'=4,'ctx_1'=8,'head_0'=4,'head_1'=2] {'ctx_1'}, dimensions={0}, use_global_device_ids=true | all-gather | bytes 599040 | tf_op jit(solution)/shard_map/all_gather | solution.py:28
  160.0 8.8 %all-to-all-start.2 = ((f32[32,256,64]{1,2,0:T(8,128)}), f32[32,256,64]{1,2,0:T(8,128)}, u32[]{:S(2)}, u32[]{:S(2)}) async-start(f32[32,256,64]{1,2,0:T(8,128)} %convolution_bitcast_fusion), calls=%async_computation.2 | async-start | bytes 4194304 | tf_op jit(solution)/shard_map/all_to_all | solution.py:101
  168.9 13.9 %all_gather.42 = bf16[4,256,256]{2,1,0:T(8,128)(2,1)} all-gather(bf16[1,256,256]{2,1,0:T(8,128)(2,1)} %copy.125), channel_id=1, replica_groups=mesh['ctx_0'=4,'ctx_1'=8,'head_0'=4,'head_1'=2] {'head_0'}, dimensions={0}, use_global_device_ids=true | all-gather | bytes 655360 | tf_op jit(solution)/shard_map/all_gather | solution.py:60
  189.7 4.4 %slice_add_fusion.28 = (f32[1,1,128]{2,1,0:T(1,128)S(1)}, f32[1,1,128]{2,1,0:T(1,128)S(1)}, f32[1,1,128]{2,1,0:T(1,128)S(1)}) fusion(f32[8,130,128]{2,1,0:T(8,128)S(1)} %all-gather.6, f32[]{:T(128)} %bitcast.115, f32[]{:T(128)} %bitcast.116, f32[]{:T(128)} %bitcast.118, f32[]{:T(128)} %bitcast.117, f32[]{:T(128)} %bitcast.122, f32[]{:T(128)} %bitcast.121, ...), kind=kLoop, calls=%fused_computation.167 | loop fusion | flops 1920 | bytes 5664 | tf_op jit(solution)/shard_map/add | solution.py:151
  194.1 5.0 %slice_add_fusion.4 = (f32[1,128,128]{2,1,0:T(8,128)S(1)}, f32[1,128,128]{2,1,0:T(8,128)}) fusion(f32[8,130,128]{2,1,0:T(8,128)S(1)} %all-gather.6, f32[]{:T(128)} %bitcast.116, f32[]{:T(128)} %bitcast.115, f32[]{:T(128)} %bitcast.118, f32[]{:T(128)} %bitcast.117, f32[]{:T(128)} %bitcast.122, f32[]{:T(128)} %bitcast.121, f32[]{:T(128)} %bitcast.120, ...), kind=kLoop, calls=%fused_computation.104 | loop fusion | flops 245760 | bytes 655392 | tf_op jit(solution)/shard_map/add | solution.py:150
  199.8 12.5 %all-gather.7 = f32[4,130,128]{2,1,0:T(8,128)S(1)} all-gather(f32[1,130,128]{2,1,0:T(8,128)S(1)} %maximum_bitcast_fusion.7), channel_id=5, replica_groups=mesh['ctx_0'=4,'ctx_1'=8,'head_0'=4,'head_1'=2] {'ctx_0'}, dimensions={0}, use_global_device_ids=true | all-gather | bytes 332800 | tf_op jit(solution)/shard_map/all_gather | solution.py:28
  214.3 1.7 copy.124
  215.9 3.6 %all_gather.40 = bf16[2,256,256]{2,1,0:T(8,128)(2,1)} all-gather(bf16[1,256,256]{2,1,0:T(8,128)(2,1)} %copy.124), channel_id=1, replica_groups=mesh['ctx_0'=4,'ctx_1'=8,'head_0'=4,'head_1'=2] {'head_1'}, dimensions={0}, use_global_device_ids=true | all-gather | bytes 393216 | tf_op jit(solution)/shard_map/all_gather | solution.py:60
  219.6 1.7 multiply_reduce_fusion
  225.6 2.1 copy.145
  227.6 6.1 %fusion.66 = f32[128,128]{1,0:T(8,128)S(1)} fusion(f32[4,130,128]{2,1,0:T(8,128)} %copy-done.10, f32[1,128,128]{2,1,0:T(8,128)} %copy-done.16, f32[1,128,128]{2,1,0:T(8,128)} %get-tuple-element.39, f32[8,130,128]{2,1,0:T(8,128)S(1)} %all-gather.6, f32[]{:T(128)} %bitcast.131, f32[]{:T(128)} %bitcast.130, f32[]{:T(128)} %bitcast.129, f32[]{:T(128)} %bitcast.128, ...), kind=kLoop, calls=%fused_computation.100 | loop fusion | flops 524288 | bytes 852024 | tf_op jit(solution)/shard_map/reshape.221
  233.7 2.0 fusion.23
  236.2 5.1 %bitcast_add_fusion.1 = f32[128]{0:T(128)S(1)} fusion(f32[1,1,128]{2,1,0:T(1,128)S(1)} %get-tuple-element.40, f32[1,1,128]{2,1,0:T(1,128)S(1)} %get-tuple-element.41, f32[1,1,128]{2,1,0:T(1,128)S(1)} %get-tuple-element.42, pred[]{:T(512)} %lt.62, pred[]{:T(512)} %lt.61, pred[]{:T(512)} %lt.60, pred[]{:T(512)} %lt.59, pred[]{:T(512)} %lt.58, pred[]{:T(512)} %lt.57, ...), kind=kLoop, calls=%fused_computation.189 | loop fusion | flops 3840 | bytes 6708 | tf_op jit(solution)/shard_map/add | solution.py:151
  244.2 2.5 all-gather.11.cloned.1.call-done
  246.8 2.9 %fusion.13 = bf16[512,256]{1,0:T(8,128)(2,1)} fusion(bf16[8,256,256]{2,1,0:T(8,128)(2,1)S(1)} %bitcast.355, bf16[8,256,256]{2,1,0:T(8,128)(2,1)} %all-gather.11.cloned.1.call-done, bf16[256,8,256]{2,0,1:T(8,128)(2,1)} %all-to-all-done), kind=kOutput, calls=%fused_computation.25 | convolution fusion | flops 541196288 | bytes 3407872 | tf_op jit(solution)/shard_map/dot_general | solution.py:227
  249.7 2.3 reduce_sum.86
  (105 shorter events, 27.6 us)
Async XLA Ops:
  7.2 8.0 %copy-start = (bf16[512,128]{1,0:T(8,128)(2,1)S(1)}, bf16[512,128]{1,0:T(8,128)(2,1)}, u32[]{:S(2)}) copy-start(bf16[512,128]{1,0:T(8,128)(2,1)} %param.9) | copy-start | bytes 393220
  9.8 5.2 %copy-start.9 = (bf16[512,128]{1,0:T(8,128)(2,1)S(1)}, bf16[512,128]{1,0:T(8,128)(2,1)}, u32[]{:S(2)}) copy-start(bf16[512,128]{1,0:T(8,128)(2,1)} %param.8) | copy-start | bytes 393220
  9.8 92.9 %all-to-all-start.1 = ((bf16[8,512,256]{1,2,0:T(8,128)(2,1)}), bf16[8,512,256]{1,2,0:T(8,128)(2,1)S(1)}, u32[]{:S(2)}, u32[]{:S(2)}) async-start(bf16[8,512,256]{1,2,0:T(8,128)(2,1)} %broadcast_in_dim.34), calls=%async_computation.1 | async-start | bytes 4194304 | tf_op jit(solution)/shard_map/all_to_all | solution.py:87
  14.3 59.6 %copy-start.12 = (bf16[512,256]{1,0:T(8,128)(2,1)S(1)}, bf16[512,256]{1,0:T(8,128)(2,1)}, u32[]{:S(2)}) copy-start(bf16[512,256]{1,0:T(8,128)(2,1)} %param.7) | copy-start | bytes 786436
  44.8 6.2 %copy-start.7 = (f32[8,130,128]{2,1,0:T(8,128)}, f32[8,130,128]{2,1,0:T(8,128)S(1)}, u32[]{:S(2)}) copy-start(f32[8,130,128]{2,1,0:T(8,128)S(1)} %all-gather.4) | copy-start | bytes 1597444
  51.0 24.0 %copy-start.15 = (f32[1,128,128]{2,1,0:T(8,128)}, f32[1,128,128]{2,1,0:T(8,128)S(1)}, u32[]{:S(2)}) copy-start(f32[1,128,128]{2,1,0:T(8,128)S(1)} %get-tuple-element.46) | copy-start | bytes 196612
  73.1 0.7 copy-start.11
  75.0 24.1 %copy-start.5 = (f32[64,2,8,128]{3,2,1,0:T(8,128)}, f32[64,2,8,128]{3,2,1,0:T(8,128)S(1)}, u32[]{:S(2)}) copy-start(f32[64,2,8,128]{3,2,1,0:T(8,128)S(1)} %get-tuple-element.55) | copy-start | bytes 1572868
  92.9 7.8 %copy-start.13 = (bf16[512,256]{1,0:T(8,128)(2,1)S(1)}, bf16[512,256]{1,0:T(8,128)(2,1)}, u32[]{:S(2)}) copy-start(bf16[512,256]{1,0:T(8,128)(2,1)} %param.7) | copy-start | bytes 786436
  100.8 0.9 copy-start.23
  101.3 1.4 copy-start.1
  101.7 7.6 %copy-start.21 = (f32[2]{0:T(128)}, f32[2]{0:T(128)S(1)}, u32[]{:S(2)}) copy-start(f32[2]{0:T(128)S(1)} %get-tuple-element.51) | copy-start | bytes 28
  102.7 20.5 %all-to-all-start = ((bf16[256,8,256]{2,0,1:T(8,128)(2,1)}), bf16[256,8,256]{2,0,1:T(8,128)(2,1)}, u32[]{:S(2)}, u32[]{:S(2)}) async-start(bf16[256,8,256]{2,0,1:T(8,128)(2,1)} %copy.128), calls=%async_computation | async-start | bytes 2097152 | tf_op jit(solution)/shard_map/all_to_all | solution.py:226
  107.1 2.1 copy-start.2
  107.1 2.1 copy-start.17
  109.2 0.8 copy-start.18
  109.3 1.3 copy-start.6
  123.8 36.2 %all-to-all-start.3 = ((f32[32,1,2]{2,1,0:T(1,128)}), f32[32,1,2]{2,1,0:T(1,128)S(1)}, u32[]{:S(2)}, u32[]{:S(2)}) async-start(f32[32,1,2]{2,1,0:T(1,128)} %broadcast_in_dim.35), calls=%async_computation.3 | async-start | bytes 32768 | tf_op jit(solution)/shard_map/all_to_all | solution.py:87
  160.0 89.7 %all-to-all-start.2 = ((f32[32,256,64]{1,2,0:T(8,128)}), f32[32,256,64]{1,2,0:T(8,128)}, u32[]{:S(2)}, u32[]{:S(2)}) async-start(f32[32,256,64]{1,2,0:T(8,128)} %convolution_bitcast_fusion), calls=%async_computation.2 | async-start | bytes 4194304 | tf_op jit(solution)/shard_map/all_to_all | solution.py:101
  168.8 50.8 %copy-start.3 = (f32[1,1,2,512,512]{3,4,2,1,0:T(8,128)S(1)}, f32[1,1,2,512,512]{3,4,2,1,0:T(8,128)}, u32[]{:S(2)}) copy-start(f32[1,1,2,512,512]{3,4,2,1,0:T(8,128)} %copy-done.1) | copy-start | bytes 6291460
  168.8 74.1 %all-gather.13.cloned.1.call-start = ((), (), s32[]{:S(2)}) async-start(), calls=%async_computation.5 | async-start | bytes 1572864 | tf_op jit(solution)/shard_map/all_gather | solution.py:60
  182.8 64.0 %all-gather.11.cloned.1.call-start = ((), (), s32[]{:S(2)}) async-start(), calls=%async_computation.4 | async-start | bytes 1310720 | tf_op jit(solution)/shard_map/all_gather | solution.py:60
  199.1 0.6 copy-start.16
  212.3 0.7 copy-start.10
  219.6 1.7 copy-start.4
  219.6 1.7 copy-start.22
  221.4 1.0 copy-start.19
  222.9 1.2 copy-start.8
  222.9 1.2 copy-start.20
  225.6 10.2 %copy-start.14 = (bf16[512,256]{1,0:T(8,128)(2,1)S(1)}, bf16[512,256]{1,0:T(8,128)(2,1)}, u32[]{:S(2)}) copy-start(bf16[512,256]{1,0:T(8,128)(2,1)} %param.7) | copy-start | bytes 786436
Sparse Core Ops, SparseCore 0:
  182.9 13.7 all-gather.12
  219.7 26.9 all-gather.10
where the time goes:
time: 261 us; the launch traced here: 259 us
  blocking collectives  98.7 us (38%)
  other arithmetic  47.8 us (18%)
  between operations  29 us (11%)
  local copies, waits for them, and re-layouts  26.1 us (10%)
  starting transfers between devices  25.5 us (10%)
  matrix products  20.5 us (8%)
  waiting for transfers between devices  11.3 us (4%)
    all_gather x4, blocking collectives, collected_together(): both, at, found = (lax.all_gather(jnp.concatenate(lines), axis), 0, {})  81.2 us
    add x4, other arithmetic, compose(): later[2][:, None] * earlier[1] + later[1]  19.5 us
    all_gather x2, blocking collectives, gather_in_order(): parts = lax.all_gather(parts, axes[k], axis=0, tiled=True)  17.5 us
    another operation x3, other arithmetic  12.9 us
    all_to_all x2, starting transfers between devices, copy_for_each(): return lax.all_to_all(copies, axis, split_axis=0, concat_axis=0, tiled=True)  12.2 us
    add x2, other arithmetic, compose(): later[2][:, None, None] * earlier[0] + later[0]  9.96 us
    all_to_all x1, starting transfers between devices, sent_and_summed(): lax.all_to_all(parts, axis, split_axis=0, concat_axis=0, tiled=True)  8.76 us
    all_to_all x1, waiting for transfers between devices, body(): lax.all_to_all(out_weight, HEAD, split_axis=1, concat_axis=0, tiled=True)  8.74 us
  transfers between devices with their start and end apart: 6, of which 2 were waited for; matrix products, arithmetic and copies ran while one was open for 33% of the time, Pallas kernels for 0%

commit v1 on v0

--- a/solution.py
+++ b/solution.py
@@ -9,6 +9,18 @@
 CTX = ("ctx_0", "ctx_1")
 HEAD = ("head_0", "head_1")
 highest = lax.Precision.HIGHEST
+
+
+def create_numbers(xx, named_axis):
+    return jnp.concatenate(
+        lax.all_to_all(
+            jnp.stack([xx for _ in range(lax.axis_size(named_axis))], axis=0),
+            axis_name=named_axis,
+            split_axis=0,
+            concat_axis=0,
+        ),
+        0,
+    )
 
 
 def neutral_like(value, identity):
@@ -57,7 +69,7 @@
 def gather_in_order(value, axes, order):
     parts = value[None]
     for k in order:
-        parts = lax.all_gather(parts, axes[k], axis=0, tiled=True)
+        parts = create_numbers(parts, axes[k])
     current = [lax.axis_size(axes[k]) for k in reversed(order)]
     parts = parts.reshape(*current, *value.shape)
     turned = sorted(range(len(order)), key=lambda place: order[len(order) - 1 - place])

time: 261 us -> 319 us (1.22)
  blocking collectives: 98.7 us -> 135 us
  waiting for transfers between devices: 11.3 us -> 30.3 us
  between operations: 29 us -> 16 us
  starting transfers between devices: 25.5 us -> 30.9 us
  matrix products: 20.5 us -> 24.5 us
  other arithmetic: 47.8 us -> 51.2 us
    all_gather x4, blocking collectives: 81.2 us -> 122 us  [collected_together(): both, at, found = (lax.all_gather(jnp.concatenate(lines), axis), 0, {})]
    all_gather x2 -> x0, blocking collectives: 17.5 us -> none  [gather_in_order(): parts = lax.all_gather(parts, axes[k], axis=0, tiled=True)]
    all_to_all x0 -> x2, waiting for transfers between devices: none -> 16.3 us  [create_numbers(): lax.all_to_all(jnp.stack([xx for _ in range(lax.axis_size(named_axis))],...]
    all_to_all x0 -> x2, blocking collectives: none -> 12.5 us  [create_numbers(): lax.all_to_all(jnp.stack([xx for _ in range(lax.axis_size(named_axis))],...]
    all_to_all x0 -> x2, starting transfers between devices: none -> 8.45 us  [create_numbers(): lax.all_to_all(jnp.stack([xx for _ in range(lax.axis_size(named_axis))],...]
    another operation x0 -> x4, local copies, waits for them, and re-layouts: none -> 6.28 us  [create_numbers(): jnp.stack([xx for _ in range(lax.axis_size(named_axis))], axis=0)]
    all_to_all x2, waiting for transfers between devices: 0.01 us -> 6.24 us  [copy_for_each(): return lax.all_to_all(copies, axis, split_axis=0, concat_axis=0, tiled=True)]
    broadcast_in_dim x2 -> x0, local copies, waits for them, and re-layouts: 3.33 us -> none  [gather_in_order(): parts = value[None]]
  transfers between devices with their start and end apart: 6 -> 6, of which waited for: 2 -> 4; matrix products, arithmetic and copies ran while one was open for 33% -> 29% of each run, Pallas kernels for 0% -> 0%
where the time goes in v1:
time: 319 us; the launch traced here: 317 us
  blocking collectives  135 us (42%)
  other arithmetic  51.2 us (16%)
  starting transfers between devices  30.9 us (10%)
  waiting for transfers between devices  30.3 us (9%)
  local copies, waits for them, and re-layouts  29.2 us (9%)
  matrix products  24.5 us (8%)
  between operations  16 us (5%)
    all_gather x4, blocking collectives, collected_together(): both, at, found = (lax.all_gather(jnp.concatenate(lines), axis), 0, {})  122 us
    add x4, other arithmetic, compose(): later[2][:, None] * earlier[1] + later[1]  19.7 us
    all_to_all x2, waiting for transfers between devices, create_numbers(): lax.all_to_all(jnp.stack([xx for _ in range(lax.axis_size(named_axis))],...  16.3 us
    all_to_all x2, blocking collectives, create_numbers(): lax.all_to_all(jnp.stack([xx for _ in range(lax.axis_size(named_axis))],...  12.5 us
    all_to_all x2, starting transfers between devices, copy_for_each(): return lax.all_to_all(copies, axis, split_axis=0, concat_axis=0, tiled=True)  12.2 us
    another operation x3, other arithmetic  11.9 us
    add x2, other arithmetic, compose(): later[2][:, None, None] * earlier[0] + later[0]  10.2 us
    unnamed x57, local copies, waits for them, and re-layouts  8.64 us
  transfers between devices with their start and end apart: 6, of which 4 were waited for; matrix products, arithmetic and copies ran while one was open for 29% of the time, Pallas kernels for 0%

profile of v1, /device:TPU:8, one launch (start us, length us, event | category | flops | bytes accessed | tf_op | source)
XLA Modules:
  0.0 316.9 jit_solution(15532567984805036657)
XLA Ops:
  3.3 4.4 %all-to-all-start.5 = ((bf16[8,512,256]{1,2,0:T(8,128)(2,1)}), bf16[8,512,256]{1,2,0:T(8,128)(2,1)S(1)}, u32[]{:S(2)}, u32[]{:S(2)}) async-start(bf16[8,512,256]{1,2,0:T(8,128)(2,1)} %broadcast_in_dim.24), calls=%async_computation.5 | async-start | bytes 4194304 | tf_op jit(solution)/shard_map/all_to_all | solution.py:99
  9.1 29.1 %all-gather.4 = f32[8,130,128]{2,1,0:T(8,128)S(1)} all-gather(f32[1,130,128]{2,1,0:T(8,128)S(1)} %fusion.61), channel_id=2, replica_groups=mesh['ctx_0'=4,'ctx_1'=8,'head_0'=4,'head_1'=2] {'ctx_1'}, dimensions={0}, use_global_device_ids=true | all-gather | bytes 599040 | tf_op jit(solution)/shard_map/all_gather | solution.py:40
  39.5 5.2 %slice_add_fusion.16 = (f32[1,128,128]{2,1,0:T(8,128)S(1)}, f32[1,128,128]{2,1,0:T(8,128)}) fusion(f32[8,130,128]{2,1,0:T(8,128)S(1)} %all-gather.4, f32[]{:T(128)} %bitcast.23, f32[]{:T(128)} %bitcast.22, f32[]{:T(128)} %bitcast.25, f32[]{:T(128)} %bitcast.24, f32[]{:T(128)} %bitcast.29, f32[]{:T(128)} %bitcast.28, f32[]{:T(128)} %bitcast.27, f32[]{:T(128)} %bitcast.26), kind=kLoop, calls=%fused_computation.122 | loop fusion | flops 245760 | bytes 655392 | tf_op jit(solution)/shard_map/add | solution.py:162
  44.7 4.5 %slice_add_fusion.40 = (f32[1,1,128]{2,1,0:T(1,128)S(1)}, f32[1,1,128]{2,1,0:T(1,128)S(1)}, f32[1,1,128]{2,1,0:T(1,128)S(1)}) fusion(f32[8,130,128]{2,1,0:T(8,128)S(1)} %all-gather.4, f32[]{:T(128)} %bitcast.22, f32[]{:T(128)} %bitcast.23, f32[]{:T(128)} %bitcast.25, f32[]{:T(128)} %bitcast.24, f32[]{:T(128)} %bitcast.29, f32[]{:T(128)} %bitcast.28, ...), kind=kLoop, calls=%fused_computation.181 | loop fusion | flops 1920 | bytes 5664 | tf_op jit(solution)/shard_map/add | solution.py:163
  54.5 12.8 %all-gather.5 = f32[4,130,128]{2,1,0:T(8,128)S(1)} all-gather(f32[1,130,128]{2,1,0:T(8,128)S(1)} %maximum_bitcast_fusion.6), channel_id=3, replica_groups=mesh['ctx_0'=4,'ctx_1'=8,'head_0'=4,'head_1'=2] {'ctx_0'}, dimensions={0}, use_global_device_ids=true | all-gather | bytes 332800 | tf_op jit(solution)/shard_map/all_gather | solution.py:40
  71.9 5.7 %bitcast_add_fusion.2 = (f32[128]{0:T(128)}, f32[1,1,128]{2,1,0:T(1,128)S(1)}, f32[1,1,128]{2,1,0:T(1,128)S(1)}) fusion(f32[1,1,128]{2,1,0:T(1,128)S(1)} %get-tuple-element.48, f32[1,1,128]{2,1,0:T(1,128)S(1)} %get-tuple-element.49, f32[1,1,128]{2,1,0:T(1,128)S(1)} %get-tuple-element.50, pred[]{:T(512)} %gt.71, pred[]{:T(512)} %gt.70, ...), kind=kLoop, calls=%fused_computation.192 | loop fusion | flops 3840 | bytes 7732 | tf_op jit(solution)/shard_map/add | solution.py:163
  80.6 2.3 copy.127
  82.9 2.3 copy.128
  88.4 5.1 %fusion.70 = f32[128,128,1]{1,0,2:T(8,128)S(1)} fusion(f32[4,130,128]{2,1,0:T(8,128)S(1)} %copy-done.12, f32[1,128,128]{2,1,0:T(8,128)S(1)} %copy-done.19, f32[1,128,128]{2,1,0:T(8,128)S(1)} %copy-done.22, f32[8,130,128]{2,1,0:T(8,128)S(1)} %copy-done.8, f32[]{:T(128)} %bitcast.38, f32[]{:T(128)} %bitcast.37, f32[]{:T(128)} %bitcast.36, f32[]{:T(128)} %bitcast.35, ...), kind=kLoop, calls=%fused_computation.118 | loop fusion | flops 524288 | bytes 852024 | tf_op jit(solution)/shard_map/reshape.105
  93.5 4.4 %all-to-all-start.4 = ((bf16[256,8,256]{2,0,1:T(8,128)(2,1)}), bf16[256,8,256]{2,0,1:T(8,128)(2,1)}, u32[]{:S(2)}, u32[]{:S(2)}) async-start(bf16[256,8,256]{2,0,1:T(8,128)(2,1)} %copy.128), calls=%async_computation.4 | async-start | bytes 2097152 | tf_op jit(solution)/shard_map/all_to_all | solution.py:238
  98.7 2.1 bitcast_divide_fusion
  106.3 7.7 %all-to-all-done.4 = bf16[256,8,256]{2,0,1:T(8,128)(2,1)} async-done(((bf16[256,8,256]{2,0,1:T(8,128)(2,1)}), bf16[256,8,256]{2,0,1:T(8,128)(2,1)}, u32[]{:S(2)}, u32[]{:S(2)}) %all-to-all-start.4) | async-done | bytes 1048608 | tf_op jit(solution)/shard_map/all_to_all | solution.py:238
  114.0 5.8 %all_to_all.52 = bf16[2,1,256,256]{2,3,1,0:T(8,128)(2,1)} all-to-all(bf16[2,1,256,256]{2,3,1,0:T(8,128)(2,1)} %pad_maximum_fusion.1), channel_id=1, replica_groups=mesh['ctx_0'=4,'ctx_1'=8,'head_0'=4,'head_1'=2] {'head_1'}, dimensions={0} | all-to-all | bytes 524288 | tf_op jit(solution)/shard_map/all_to_all | solution.py:16
  121.5 4.2 %all-to-all-start.2 = ((bf16[4,1,256,256]{3,2,1,0:T(8,128)(2,1)}), bf16[4,1,256,256]{3,2,1,0:T(8,128)(2,1)}, u32[]{:S(2)}, u32[]{:S(2)}) async-start(bf16[4,1,256,256]{3,2,1,0:T(8,128)(2,1)} %stack.17), calls=%async_computation.2 | async-start | bytes 1048576 | tf_op jit(solution)/shard_map/all_to_all | solution.py:16
  129.6 6.2 %all-to-all-done.2 = bf16[4,1,256,256]{3,2,1,0:T(8,128)(2,1)} async-done(((bf16[4,1,256,256]{3,2,1,0:T(8,128)(2,1)}), bf16[4,1,256,256]{3,2,1,0:T(8,128)(2,1)}, u32[]{:S(2)}, u32[]{:S(2)}) %all-to-all-start.2) | async-done | bytes 524320 | tf_op jit(solution)/shard_map/all_to_all | solution.py:16
  136.4 7.8 %all-to-all-start.7 = ((f32[32,1,2]{2,1,0:T(1,128)}), f32[32,1,2]{2,1,0:T(1,128)S(1)}, u32[]{:S(2)}, u32[]{:S(2)}) async-start(f32[32,1,2]{2,1,0:T(1,128)} %broadcast_in_dim.25), calls=%async_computation.7 | async-start | bytes 32768 | tf_op jit(solution)/shard_map/all_to_all | solution.py:99
  144.2 2.3 pad_maximum_fusion
  146.6 6.2 %all-to-all-done.7 = f32[32,1,2]{2,1,0:T(1,128)S(1)} async-done(((f32[32,1,2]{2,1,0:T(1,128)}), f32[32,1,2]{2,1,0:T(1,128)S(1)}, u32[]{:S(2)}, u32[]{:S(2)}) %all-to-all-start.7) | async-done | bytes 288 | tf_op jit(solution)/shard_map/all_to_all | solution.py:99
  152.8 6.7 %all_to_all.53 = bf16[2,4,256,256]{3,2,1,0:T(8,128)(2,1)} all-to-all(bf16[2,4,256,256]{3,2,1,0:T(8,128)(2,1)} %pad_maximum_fusion), channel_id=1, replica_groups=mesh['ctx_0'=4,'ctx_1'=8,'head_0'=4,'head_1'=2] {'head_1'}, dimensions={0} | all-to-all | bytes 2097152 | tf_op jit(solution)/shard_map/all_to_all | solution.py:16
  160.6 4.3 %all-to-all-start.1 = ((bf16[4,2,256,256]{3,2,1,0:T(8,128)(2,1)}), bf16[4,2,256,256]{3,2,1,0:T(8,128)(2,1)}, u32[]{:S(2)}, u32[]{:S(2)}) async-start(bf16[4,2,256,256]{3,2,1,0:T(8,128)(2,1)} %stack.16), calls=%async_computation.1 | async-start | bytes 2097152 | tf_op jit(solution)/shard_map/all_to_all | solution.py:16
  167.6 3.0 convolution_bitcast_fusion
  170.6 10.1 %all-to-all-done.1 = bf16[4,2,256,256]{3,2,1,0:T(8,128)(2,1)} async-done(((bf16[4,2,256,256]{3,2,1,0:T(8,128)(2,1)}), bf16[4,2,256,256]{3,2,1,0:T(8,128)(2,1)}, u32[]{:S(2)}, u32[]{:S(2)}) %all-to-all-start.1) | async-done | bytes 1048608 | tf_op jit(solution)/shard_map/all_to_all | solution.py:16
  180.6 5.8 %all-to-all-start.6 = ((f32[32,256,64]{1,2,0:T(8,128)}), f32[32,256,64]{1,2,0:T(8,128)}, u32[]{:S(2)}, u32[]{:S(2)}) async-start(f32[32,256,64]{1,2,0:T(8,128)} %convolution_bitcast_fusion), calls=%async_computation.6 | async-start | bytes 4194304 | tf_op jit(solution)/shard_map/all_to_all | solution.py:113
  186.5 68.0 %all-gather.6 = f32[8,130,128]{2,1,0:T(8,128)S(1)} all-gather(f32[1,130,128]{2,1,0:T(8,128)} %fusion.62), channel_id=4, replica_groups=mesh['ctx_0'=4,'ctx_1'=8,'head_0'=4,'head_1'=2] {'ctx_1'}, dimensions={0}, use_global_device_ids=true | all-gather | bytes 599040 | tf_op jit(solution)/shard_map/all_gather | solution.py:40
  261.4 4.4 %slice_add_fusion.28 = (f32[1,1,128]{2,1,0:T(1,128)S(1)}, f32[1,1,128]{2,1,0:T(1,128)S(1)}, f32[1,1,128]{2,1,0:T(1,128)S(1)}) fusion(f32[8,130,128]{2,1,0:T(8,128)S(1)} %all-gather.6, f32[]{:T(128)} %bitcast.117, f32[]{:T(128)} %bitcast.118, f32[]{:T(128)} %bitcast.120, f32[]{:T(128)} %bitcast.119, f32[]{:T(128)} %bitcast.124, f32[]{:T(128)} %bitcast.123, ...), kind=kLoop, calls=%fused_computation.169 | loop fusion | flops 1920 | bytes 5664 | tf_op jit(solution)/shard_map/add | solution.py:163
  265.7 5.0 %slice_add_fusion.4 = (f32[1,128,128]{2,1,0:T(8,128)S(1)}, f32[1,128,128]{2,1,0:T(8,128)}) fusion(f32[8,130,128]{2,1,0:T(8,128)S(1)} %all-gather.6, f32[]{:T(128)} %bitcast.118, f32[]{:T(128)} %bitcast.117, f32[]{:T(128)} %bitcast.120, f32[]{:T(128)} %bitcast.119, f32[]{:T(128)} %bitcast.124, f32[]{:T(128)} %bitcast.123, f32[]{:T(128)} %bitcast.122, ...), kind=kLoop, calls=%fused_computation.106 | loop fusion | flops 245760 | bytes 655392 | tf_op jit(solution)/shard_map/add | solution.py:162
  271.4 12.6 %all-gather.7 = f32[4,130,128]{2,1,0:T(8,128)S(1)} all-gather(f32[1,130,128]{2,1,0:T(8,128)S(1)} %maximum_bitcast_fusion.7), channel_id=5, replica_groups=mesh['ctx_0'=4,'ctx_1'=8,'head_0'=4,'head_1'=2] {'ctx_0'}, dimensions={0}, use_global_device_ids=true | all-gather | bytes 332800 | tf_op jit(solution)/shard_map/all_gather | solution.py:40
  285.9 2.2 fusion.12
  296.3 6.1 %fusion.66 = f32[128,128]{1,0:T(8,128)S(1)} fusion(f32[4,130,128]{2,1,0:T(8,128)} %copy-done.13, f32[1,128,128]{2,1,0:T(8,128)} %copy-done.20, f32[1,128,128]{2,1,0:T(8,128)} %get-tuple-element.39, f32[8,130,128]{2,1,0:T(8,128)S(1)} %all-gather.6, f32[]{:T(128)} %bitcast.133, f32[]{:T(128)} %bitcast.132, f32[]{:T(128)} %bitcast.131, f32[]{:T(128)} %bitcast.130, ...), kind=kLoop, calls=%fused_computation.102 | loop fusion | flops 524288 | bytes 852024 | tf_op jit(solution)/shard_map/reshape.222
  304.8 5.1 %bitcast_add_fusion.1 = f32[128]{0:T(128)S(1)} fusion(f32[1,1,128]{2,1,0:T(1,128)S(1)} %get-tuple-element.40, f32[1,1,128]{2,1,0:T(1,128)S(1)} %get-tuple-element.41, f32[1,1,128]{2,1,0:T(1,128)S(1)} %get-tuple-element.42, pred[]{:T(512)} %lt.62, pred[]{:T(512)} %lt.61, pred[]{:T(512)} %lt.60, pred[]{:T(512)} %lt.59, pred[]{:T(512)} %lt.58, pred[]{:T(512)} %lt.57, ...), kind=kLoop, calls=%fused_computation.191 | loop fusion | flops 3840 | bytes 6708 | tf_op jit(solution)/shard_map/add | solution.py:163
  311.6 3.0 fusion.13
  314.5 2.3 reduce_sum.86
  (113 shorter events, 44.2 us)
Async XLA Ops:
  0.6 8.0 %copy-start = (bf16[512,128]{1,0:T(8,128)(2,1)S(1)}, bf16[512,128]{1,0:T(8,128)(2,1)}, u32[]{:S(2)}) copy-start(bf16[512,128]{1,0:T(8,128)(2,1)} %param.9) | copy-start | bytes 393220
  3.3 5.2 %copy-start.10 = (bf16[512,128]{1,0:T(8,128)(2,1)S(1)}, bf16[512,128]{1,0:T(8,128)(2,1)}, u32[]{:S(2)}) copy-start(bf16[512,128]{1,0:T(8,128)(2,1)} %param.8) | copy-start | bytes 393220
  3.3 90.3 %all-to-all-start.5 = ((bf16[8,512,256]{1,2,0:T(8,128)(2,1)}), bf16[8,512,256]{1,2,0:T(8,128)(2,1)S(1)}, u32[]{:S(2)}, u32[]{:S(2)}) async-start(bf16[8,512,256]{1,2,0:T(8,128)(2,1)} %broadcast_in_dim.24), calls=%async_computation.5 | async-start | bytes 4194304 | tf_op jit(solution)/shard_map/all_to_all | solution.py:99
  7.7 60.3 %copy-start.16 = (bf16[512,256]{1,0:T(8,128)(2,1)S(1)}, bf16[512,256]{1,0:T(8,128)(2,1)}, u32[]{:S(2)}) copy-start(bf16[512,256]{1,0:T(8,128)(2,1)} %param.7) | copy-start | bytes 786436
  38.2 6.5 %copy-start.7 = (f32[8,130,128]{2,1,0:T(8,128)}, f32[8,130,128]{2,1,0:T(8,128)S(1)}, u32[]{:S(2)}) copy-start(f32[8,130,128]{2,1,0:T(8,128)S(1)} %all-gather.4) | copy-start | bytes 1597444
  44.7 24.4 %copy-start.18 = (f32[1,128,128]{2,1,0:T(8,128)}, f32[1,128,128]{2,1,0:T(8,128)S(1)}, u32[]{:S(2)}) copy-start(f32[1,128,128]{2,1,0:T(8,128)S(1)} %get-tuple-element.46) | copy-start | bytes 196612
  67.3 0.7 copy-start.11
  69.1 28.8 %copy-start.5 = (f32[64,2,8,128]{3,2,1,0:T(8,128)}, f32[64,2,8,128]{3,2,1,0:T(8,128)S(1)}, u32[]{:S(2)}) copy-start(f32[64,2,8,128]{3,2,1,0:T(8,128)S(1)} %get-tuple-element.55) | copy-start | bytes 1572868
  85.4 2.0 copy-start.26
  85.4 3.0 copy-start.8
  85.4 3.0 copy-start.12
  85.4 3.0 copy-start.19
  85.4 3.0 copy-start.22
  87.0 1.3 copy-start.1
  87.4 13.4 %copy-start.24 = (f32[2]{0:T(128)}, f32[2]{0:T(128)S(1)}, u32[]{:S(2)}) copy-start(f32[2]{0:T(128)S(1)} %get-tuple-element.51) | copy-start | bytes 28
  93.5 20.5 %all-to-all-start.4 = ((bf16[256,8,256]{2,0,1:T(8,128)(2,1)}), bf16[256,8,256]{2,0,1:T(8,128)(2,1)}, u32[]{:S(2)}, u32[]{:S(2)}) async-start(bf16[256,8,256]{2,0,1:T(8,128)(2,1)} %copy.128), calls=%async_computation.4 | async-start | bytes 2097152 | tf_op jit(solution)/shard_map/all_to_all | solution.py:238
  98.6 2.1 copy-start.2
  100.7 0.7 copy-start.21
  101.5 0.7 copy-start.14
  121.5 14.3 %all-to-all-start.2 = ((bf16[4,1,256,256]{3,2,1,0:T(8,128)(2,1)}), bf16[4,1,256,256]{3,2,1,0:T(8,128)(2,1)}, u32[]{:S(2)}, u32[]{:S(2)}) async-start(bf16[4,1,256,256]{3,2,1,0:T(8,128)(2,1)} %stack.17), calls=%async_computation.2 | async-start | bytes 1048576 | tf_op jit(solution)/shard_map/all_to_all | solution.py:16
  136.4 16.3 %all-to-all-start.7 = ((f32[32,1,2]{2,1,0:T(1,128)}), f32[32,1,2]{2,1,0:T(1,128)S(1)}, u32[]{:S(2)}, u32[]{:S(2)}) async-start(f32[32,1,2]{2,1,0:T(1,128)} %broadcast_in_dim.25), calls=%async_computation.7 | async-start | bytes 32768 | tf_op jit(solution)/shard_map/all_to_all | solution.py:99
  152.8 6.7 %copy-start.15 = (bf16[2,256,256]{2,1,0:T(8,128)(2,1)S(1)}, bf16[2,256,256]{2,1,0:T(8,128)(2,1)}, u32[]{:S(2)}) copy-start(bf16[2,256,256]{2,1,0:T(8,128)(2,1)} %copy.124) | copy-start | bytes 786436
  160.6 20.0 %all-to-all-start.1 = ((bf16[4,2,256,256]{3,2,1,0:T(8,128)(2,1)}), bf16[4,2,256,256]{3,2,1,0:T(8,128)(2,1)}, u32[]{:S(2)}, u32[]{:S(2)}) async-start(bf16[4,2,256,256]{3,2,1,0:T(8,128)(2,1)} %stack.16), calls=%async_computation.1 | async-start | bytes 2097152 | tf_op jit(solution)/shard_map/all_to_all | solution.py:16
  170.6 115.4 %copy-start.3 = (f32[1,1,2,512,512]{3,4,2,1,0:T(8,128)S(1)}, f32[1,1,2,512,512]{3,4,2,1,0:T(8,128)}, u32[]{:S(2)}) copy-start(f32[1,1,2,512,512]{3,4,2,1,0:T(8,128)} %copy-done.1) | copy-start | bytes 6291460
  180.6 133.9 %all-to-all-start.6 = ((f32[32,256,64]{1,2,0:T(8,128)}), f32[32,256,64]{1,2,0:T(8,128)}, u32[]{:S(2)}, u32[]{:S(2)}) async-start(f32[32,256,64]{1,2,0:T(8,128)} %convolution_bitcast_fusion), calls=%async_computation.6 | async-start | bytes 4194304 | tf_op jit(solution)/shard_map/all_to_all | solution.py:113
  284.0 0.7 copy-start.13
  289.9 1.7 copy-start.4
  289.9 1.7 copy-start.25
  291.7 1.0 copy-start.9
  291.7 1.0 copy-start.23
  294.2 10.2 %copy-start.17 = (bf16[512,256]{1,0:T(8,128)(2,1)S(1)}, bf16[512,256]{1,0:T(8,128)(2,1)}, u32[]{:S(2)}) copy-start(bf16[512,256]{1,0:T(8,128)(2,1)} %param.7) | copy-start | bytes 786436
  296.3 15.2 %copy-start.6 = (bf16[2,4,256,256]{3,2,1,0:T(8,128)(2,1)S(1)}, bf16[2,4,256,256]{3,2,1,0:T(8,128)(2,1)}, u32[]{:S(2)}) copy-start(bf16[2,4,256,256]{3,2,1,0:T(8,128)(2,1)} %all_to_all.53) | copy-start | bytes 3145732
  (1 other events, 0.6 us)
